TPU v7x, 256 devices: a whole 4x4x8 slice. The times are simulated.
256 devices in a mesh: dp: 32 (over z, x_hi, core), row: 4 (over y), col: 2 (over x_lo).
Axes of the slice: x: 4 (x_hi: 2, x_lo: 2; x = x_hi * 2 + x_lo), y: 4, z: 8, core: 2. Of those that a mesh axis runs over, the one named last changes fastest.
Arguments:
- tokens: bfloat16 [6144, 4096], P('dp', ('row', 'col')), may hold values from -6 to 6
- in_weight: bfloat16 [4096, 3, 4096], P('dp', None, ('row', 'col')), may hold values from -0.09375 to 0.09375
- short_filter: float32 [3, 3, 4096], P(None, None, ('row', 'col')), may hold values from -3 to 3
- long_filter: bfloat16 [256, 128], P(('row', 'col')), may hold values from -0.59765625 to 0.59765625
- grad_out: bfloat16 [6144, 4096], P('dp', ('row', 'col')), may hold values from -6 to 6
Outputs:
- mixed: bfloat16 [6144, 4096], P('dp', ('row', 'col'))
- grad_in: bfloat16 [6144, 4096], P('dp', ('row', 'col'))
- grad_weight: float32 [4096, 3, 4096], P('dp', None, ('row', 'col'))
- grad_long: float32 [256, 128], P(('row', 'col'))
- grad_short: float32 [3, 3, 4096], P(None, None, ('row', 'col'))
All inputs are finite; a program needn't handle non-finite values.
Results may differ from a plain program's by a relative error of at most 0.019.
Values may be sent and summed in bfloat16 or wider, within the bound.
A program may use at most 128 MiB of HBM per device.

v0:
```python
import jax
import jax.numpy as jnp
from jax import lax
from jax.sharding import PartitionSpec as P


def from_behind(block, axis, distance):
    devices = range(lax.axis_size(axis))
    route = [(i - distance, i) for i in devices if i - distance in devices]
    return lax.ppermute(block, axis, route)


def toeplitz(leading, rows, span):
    groups = leading.shape[0]
    width = rows + span
    seed_row = jnp.concatenate(
        [leading, jnp.zeros((groups, width - leading.shape[1]), leading.dtype)], axis=1
    )
    tiled = jnp.tile(seed_row, (1, rows))
    skewed = tiled[:, : rows * (width - 1)].reshape(groups, rows, width - 1)
    return skewed[:, :, :span]


def to_groups(values, ngroups, members):
    count = values.shape[0]
    return values.reshape(count, ngroups, members).transpose(1, 2, 0)


def from_groups(values):
    groups, members, count = values.shape
    return values.transpose(2, 0, 1).reshape(count, groups * members)


def per_device(tokens, in_weight, short_filter, long_filter, grad_out):
    rows = tokens.shape[0]
    local = grad_out.shape[1]
    nshort = short_filter.shape[0]
    ntaps = long_filter.shape[1]
    ngroups = long_filter.shape[0]
    members = local // ngroups
    margin = ntaps - 1
    span = rows + margin
    scale = float(rows * lax.axis_size("dp")) ** (-0.5)
    whole = lax.all_gather(tokens, ("row", "col"), axis=1, tiled=True)
    full_w = lax.all_gather(in_weight, "dp", axis=0, tiled=True)
    mixed_in = jnp.einsum("sd,dic->sic", whole, full_w, preferred_element_type=jnp.float32).astype(
        jnp.bfloat16
    )
    before = from_behind(mixed_in[rows - margin - nshort + 1 :], "dp", 1)
    extended = jnp.concatenate([before, mixed_in], axis=0).astype(jnp.float32)
    long_feats = jnp.zeros((span, 3, local), jnp.float32)
    for j in range(nshort):
        long_feats = (
            long_feats + short_filter[j][None] * extended[nshort - 1 - j : nshort - 1 - j + span]
        )
    product_ext = (long_feats[:, 1] * long_feats[:, 2]).astype(jnp.bfloat16)
    feats = long_feats[margin:]
    short_rows = extended[margin:]
    product_cols = to_groups(product_ext, ngroups, members)
    causal = toeplitz(long_filter[:, ::-1], rows, span)
    conv = from_groups(
        jnp.einsum("gst,gct->gcs", causal, product_cols, preferred_element_type=jnp.float32)
    )
    mixed = (feats[:, 0] * conv).astype(jnp.bfloat16)
    upstream = grad_out.astype(jnp.float32)
    grad_query = upstream * conv
    grad_conv = (upstream * feats[:, 0]).astype(jnp.bfloat16)
    after = from_behind(grad_conv[:margin], "dp", -1)
    grad_ext = jnp.concatenate([grad_conv, after], axis=0)
    anti = toeplitz(long_filter, rows, span)
    grad_product = from_groups(
        jnp.einsum(
            "gst,gct->gcs",
            anti,
            to_groups(grad_ext, ngroups, members),
            preferred_element_type=jnp.float32,
        )
    )
    reversed_cols = jnp.concatenate(
        [product_cols[:, :, ::-1], jnp.zeros((ngroups, members, rows), product_cols.dtype)], axis=2
    )
    width = span + rows
    pairs = jnp.einsum(
        "gcs,gcu->gsu",
        to_groups(grad_conv, ngroups, members),
        reversed_cols,
        preferred_element_type=jnp.float32,
    )
    diagonal = pairs.reshape(ngroups, rows * width)[:, : rows * (width - 1)].reshape(
        ngroups, rows, width - 1
    )
    filter_part = jnp.sum(diagonal[:, :, rows - 1 : rows - 1 + ntaps], axis=1)
    grad_feats = jnp.stack(
        [grad_query, grad_product * feats[:, 2], grad_product * feats[:, 1]], axis=1
    )
    later = from_behind(grad_feats[: nshort - 1], "dp", -1)
    feats_ext = jnp.concatenate([grad_feats, later], axis=0)
    grad_acc = jnp.zeros((rows, 3, local), jnp.float32)
    for j in range(nshort):
        grad_acc = grad_acc + short_filter[j][None] * feats_ext[j : j + rows]
    grad_mixed = grad_acc.astype(jnp.bfloat16)
    short_part = jnp.stack(
        [
            jnp.sum(grad_feats * short_rows[nshort - 1 - j : nshort - 1 - j + rows], axis=0)
            for j in range(nshort)
        ]
    )
    filter_total, short_total = (
        lax.psum(filter_part.astype(jnp.bfloat16), "dp").astype(jnp.float32),
        lax.psum(short_part.astype(jnp.bfloat16), "dp").astype(jnp.float32),
    )
    grad_long = filter_total * scale
    grad_short = short_total * scale
    partial_in = jnp.einsum("sic,dic->sd", grad_mixed, full_w, preferred_element_type=jnp.float32)
    summed_in = lax.psum_scatter(
        partial_in.astype(jnp.bfloat16), ("row", "col"), scatter_dimension=1, tiled=True
    )
    weight_term = (
        jnp.einsum("sd,sic->dic", whole, grad_mixed, preferred_element_type=jnp.float32) * scale
    )
    grad_weight = lax.psum_scatter(
        weight_term.astype(jnp.bfloat16), "dp", scatter_dimension=0, tiled=True
    ).astype(jnp.float32)
    return (mixed, summed_in, grad_weight, grad_long, grad_short)


def solution(mesh):
    placed = (
        P("dp", ("row", "col")),
        P("dp", None, ("row", "col")),
        P(None, None, ("row", "col")),
        P(("row", "col"), None),
        P("dp", ("row", "col")),
    )
    return jax.shard_map(
        per_device,
        mesh=mesh,
        in_specs=placed,
        out_specs=(
            P("dp", ("row", "col")),
            P("dp", ("row", "col")),
            P("dp", None, ("row", "col")),
            P(("row", "col"), None),
            P(None, None, ("row", "col")),
        ),
        check_vma=False,
    )
```

profile of v0, /device:TPU:4, one launch (start us, length us, event | category | flops | bytes accessed | tf_op | source)
XLA Modules:
  0.0 539.4 jit_solution(406576866576352220)
XLA Ops:
  7.2 0.7 all-gather.3.cloned.1.call-update
  7.9 0.7 all-gather.5.cloned.1.call-update
  8.7 48.7 %all-gather.3.cloned.1.call-done = bf16[192,4096]{1,0:T(8,128)(2,1)} async-done(((bf16[192,512]{1,0:T(8,128)(2,1)}), bf16[192,4096]{1,0:T(8,128)(2,1)}) %all-gather.3.cloned.1.call-update) | async-done | bytes 1572880 | tf_op jit(solution)/shard_map/all_gather | solution.py:44
  57.4 117.2 %all-gather.5.cloned.1.call-done = bf16[4096,3,512]{2,0,1:T(8,128)(2,1)} async-done(((bf16[128,3,512]{2,0,1:T(8,128)(2,1)}), bf16[4096,3,512]{2,0,1:T(8,128)(2,1)}) %all-gather.5.cloned.1.call-update) | async-done | bytes 12582928 | tf_op jit(solution)/shard_map/all_gather | solution.py:45
  174.6 7.7 %fusion.10 = bf16[192,3,512]{2,0,1:T(8,128)(2,1)S(1)} fusion(bf16[4096,3,512]{2,0,1:T(8,128)(2,1)} %all-gather.5.cloned.1.call-done, bf16[192,4096]{1,0:T(8,128)(2,1)} %all-gather.3.cloned.1.call-done), kind=kOutput, calls=%fused_computation.16 | convolution fusion | flops 2416214016 | bytes 14745600 | tf_op jit(solution)/shard_map/sd,dic->sic/dot_general | solution.py:46
  182.4 2.2 collective-permute-start
  184.7 3.1 tile.8
  187.8 11.6 %tile.9 = bf16[32,98112]{1,0:T(8,128)(2,1)} reshape(bf16[32,192,511]{2,1,0:T(8,128)(2,1)} %tile.8) | data formatting | bytes 12558336 | tf_op jit(solution)/shard_map/tile | solution.py:19
  199.4 5.8 %slice.119 = bf16[32,97920]{1,0:T(8,128)(2,1)} slice(bf16[32,98112]{1,0:T(8,128)(2,1)} %tile.9), slice={[0:32], [0:97920]} | slice | bytes 12533760 | tf_op jit(solution)/shard_map/slice | solution.py:20
  205.3 15.3 %reshape.49 = bf16[32,192,510]{2,1,0:T(8,128)(2,1)} reshape(bf16[32,97920]{1,0:T(8,128)(2,1)} %slice.119) | data formatting | bytes 12533760 | tf_op jit(solution)/shard_map/reshape | solution.py:20
  220.6 0.3 maximum_convert_fusion
  220.9 0.6 fusion.5
  221.5 1.3 copy-done
  222.8 0.2 copy.24
  223.1 4.1 fusion.3
  227.2 0.9 copy.25
  228.1 1.9 fusion.23
  230.0 5.1 collective-permute-start.1
  235.2 3.2 tile.20
  238.3 11.6 %tile.21 = bf16[32,98112]{1,0:T(8,128)(2,1)} reshape(bf16[32,192,511]{2,1,0:T(8,128)(2,1)} %tile.20) | data formatting | bytes 12558336 | tf_op jit(solution)/shard_map/tile | solution.py:19
  249.9 5.8 %slice.122 = bf16[32,97920]{1,0:T(8,128)(2,1)} slice(bf16[32,98112]{1,0:T(8,128)(2,1)} %tile.21), slice={[0:32], [0:97920]} | slice | bytes 12533760 | tf_op jit(solution)/shard_map/slice | solution.py:20
  255.8 15.3 %reshape.52 = bf16[32,192,510]{2,1,0:T(8,128)(2,1)} reshape(bf16[32,97920]{1,0:T(8,128)(2,1)} %slice.122) | data formatting | bytes 12533760 | tf_op jit(solution)/shard_map/reshape | solution.py:20
  271.1 0.9 copy.27
  272.0 4.2 fusion.1
  276.2 0.9 copy.28
  277.2 1.4 slice_multiply_fusion.10
  278.7 2.0 collective-permute-start.2
  280.7 1.4 collective-permute-done.2
  282.2 0.8 fusion.15
  283.0 0.6 copy-done.6
  283.6 6.6 %multiply_convert_fusion = bf16[3,512,4096]{2,1,0:T(8,128)(2,1)} fusion(bf16[192,3,512]{2,0,1:T(8,128)(2,1)S(1)} %get-tuple-element.29, bf16[192,4096]{1,0:T(8,128)(2,1)S(1)} %copy-done.6), kind=kOutput, calls=%fused_computation | convolution fusion | flops 2428502016 | bytes 14745600 | tf_op jit(solution)/shard_map/sd,sic->dic/dot_general | solution.py:119
  290.2 16.6 %copy.34 = bf16[4096,1536]{1,0:T(8,128)(2,1)} copy(bf16[4096,1536]{0,1:T(8,128)(2,1)} %bitcast.62) | data formatting | bytes 25165824
  306.9 0.3 reduce-scatter.5.cloned.1.call-start
  307.1 0.8 copy-done.2
  307.9 10.0 %fusion = bf16[192,4096]{1,0:T(8,128)(2,1)} fusion(bf16[192,3,512]{2,0,1:T(8,128)(2,1)S(1)} %copy-done.2, bf16[4096,3,512]{2,0,1:T(8,128)(2,1)} %all-gather.5.cloned.1.call-done), kind=kOutput, calls=%fused_computation.2 | convolution fusion | flops 2416705536 | bytes 14745600 | tf_op jit(solution)/shard_map/sic,dic->sd/dot_general | solution.py:114
  318.1 0.5 reverse
  318.6 0.2 slice.183
  318.8 6.9 %fusion.20 = f32[32,192,511]{2,1,0:T(8,128)} fusion(bf16[32,16,192]{2,1,0:T(8,128)(2,1)S(1)} %bitcast.69, bf16[32,16,319]{2,1,0:T(8,128)(2,1)S(1)} %slice.183), kind=kOutput, calls=%fused_computation.33 | convolution fusion | flops 100466688 | bytes 13081600 | tf_op jit(solution)/shard_map/gcs,gcu->gsu/dot_general | solution.py:83
  325.7 13.2 %reshape.55 = f32[32,98112]{1,0:T(8,128)} reshape(f32[32,192,511]{2,1,0:T(8,128)} %fusion.20) | data formatting | bytes 25116672 | tf_op jit(solution)/shard_map/reshape | solution.py:89
  338.8 11.4 %slice.129 = f32[32,97920]{1,0:T(8,128)} slice(f32[32,98112]{1,0:T(8,128)} %reshape.55), slice={[0:32], [0:97920]} | slice | bytes 25067520 | tf_op jit(solution)/shard_map/slice | solution.py:89
  350.3 15.2 %reshape.56 = f32[32,192,510]{2,1,0:T(8,128)} reshape(f32[32,97920]{1,0:T(8,128)} %slice.129) | data formatting | bytes 25067520 | tf_op jit(solution)/shard_map/reshape | solution.py:89
  365.5 4.4 slice_reduce_fusion
  369.9 127.2 %all-reduce.3 = (bf16[32,128]{1,0:T(8,128)(2,1)S(1)}, bf16[3,3,512]{2,1,0:T(4,128)(2,1)S(1)}) all-reduce(bf16[32,128]{1,0:T(8,128)(2,1)S(1)} %slice_reduce_fusion, bf16[3,3,512]{2,1,0:T(4,128)(2,1)S(1)} %pad_maximum_fusion.3), channel_id=1, replica_groups=mesh['dp'=32,'row'=4,'col'=2] {'dp'}, use_global_device_ids=true, to_apply=%region_3.0 | all-reduce | flops 8704 | bytes 34816 | tf_op jit(solution)/shard_map/psum | solution.py:109
  497.1 0.6 convert_multiply_fusion.3
  497.8 0.6 convert_multiply_fusion.2
  498.4 1.2 copy.35
  499.6 1.1 copy.31
  500.7 32.2 %reduce-scatter.5.cloned.1.call-done = bf16[192,512]{1,0:T(8,128)(2,1)} async-done(((bf16[192,4096]{1,0:T(8,128)(2,1)}), bf16[192,512]{1,0:T(8,128)(2,1)}) %reduce-scatter.5.cloned.1.call-update) | async-done | bytes 196624 | tf_op jit(solution)/shard_map/reduce_scatter | solution.py:115
  (32 shorter events, 0.9 us)
Async XLA Ops:
  7.2 50.3 %all-gather.3.cloned.1.call-start = ((), (), s32[]{:S(2)}) async-start(), calls=%async_computation.2 | async-start | bytes 1769472 | tf_op jit(solution)/shard_map/all_gather | solution.py:44
  7.9 166.7 %all-gather.5.cloned.1.call-start = ((), (), s32[]{:S(2)}) async-start(), calls=%async_computation.3 | async-start | bytes 12976128 | tf_op jit(solution)/shard_map/all_gather | solution.py:45
  8.6 175.9 %copy-start.4 = (bf16[32,128]{1,0:T(8,128)(2,1)S(1)}, bf16[32,128]{1,0:T(8,128)(2,1)}, u32[]{:S(2)}) copy-start(bf16[32,128]{1,0:T(8,128)(2,1)} %param.8) | copy-start | bytes 24580
  8.7 489.7 %reduce-scatter.7.cloned.1.call-start = ((), (), s32[]{:S(2)}) async-start(), calls=%async_computation.5 | async-start | bytes 12976128
  182.4 38.2 %collective-permute-start = (bf16[129,3,512]{2,0,1:T(8,128)(2,1)S(1)}, bf16[129,3,512]{2,0,1:T(8,128)(2,1)S(1)}, u32[]{:S(2)}, u32[]{:S(2)}) collective-permute-start(bf16[129,3,512]{2,0,1:T(8,128)(2,1)S(1)} %slice.112), channel_id=1, source_target_pairs={{0,8},{8,16},{16,24},{24,32},{32,40},{40,48},{48,56},{56,64},{64,7... | collective-permute-start | bytes 1188872 | tf_op jit(solution)/shard_map/ppermute | solution.py:10
  205.3 15.3 %copy-start.5 = (f32[3,3,512]{2,1,0:T(4,128)S(1)}, f32[3,3,512]{2,1,0:T(4,128)}, u32[]{:S(2)}) copy-start(f32[3,3,512]{2,1,0:T(4,128)} %param.7) | copy-start | bytes 55300
  221.5 1.3 copy-start
  223.1 5.1 copy-start.3
  230.0 41.0 %collective-permute-start.1 = (bf16[127,512]{1,0:T(8,128)(2,1)S(1)}, bf16[127,512]{1,0:T(8,128)(2,1)S(1)}, u32[]{:S(2)}, u32[]{:S(2)}) collective-permute-start(bf16[127,512]{1,0:T(8,128)(2,1)S(1)} %slice.121), channel_id=1, source_target_pairs={{8,0},{16,8},{24,16},{32,24},{40,32},{48,40},{56,48},{64,56},{72,6... | collective-permute-start | bytes 390152 | tf_op jit(solution)/shard_map/ppermute | solution.py:10
  278.7 3.4 collective-permute-start.2
  282.2 1.4 copy-start.6
  283.0 7.2 %copy-start.1 = (bf16[192,3,512]{2,0,1:T(8,128)(2,1)}, bf16[192,3,512]{2,0,1:T(8,128)(2,1)S(1)}, u32[]{:S(2)}) copy-start(bf16[192,3,512]{2,0,1:T(8,128)(2,1)S(1)} %get-tuple-element.29) | copy-start | bytes 1769476
  306.8 1.1 copy-start.2
  306.9 226.0 %reduce-scatter.5.cloned.1.call-start = ((), (), s32[]{:S(2)}) async-start(), calls=%async_computation.4 | async-start | bytes 1769472 | tf_op jit(solution)/shard_map/reduce_scatter | solution.py:115
Sparse Core Ops, SparseCore 0:
  9.8 47.6 all-gather.2
  60.2 114.3 all-gather.4
  307.0 175.7 reduce-scatter.6
  485.8 47.0 reduce-scatter.4
where the time goes:
time: 540 us; the launch traced here: 539 us
  waiting for transfers between devices  201 us (37%)
  local copies, waits for them, and re-layouts  137 us (25%)
  blocking collectives  127 us (24%)
  matrix products  39.5 us (7%)
  between operations  14 us (3%)
  other arithmetic  10.9 us (2%)
  starting transfers between devices  9.64 us (2%)
    psum x1, blocking collectives, per_device(): lax.psum(filter_part.astype(jnp.bfloat16), 'dp').astype(jnp.float32)  127 us
    all_gather x1, waiting for transfers between devices, per_device(): full_w = lax.all_gather(in_weight, 'dp', axis=0, tiled=True)  117 us
    all_gather x1, waiting for transfers between devices, per_device(): whole = lax.all_gather(tokens, ('row', 'col'), axis=1, tiled=True)  48.7 us
    reduce_scatter x1, waiting for transfers between devices, per_device(): lax.psum_scatter(partial_in.astype(jnp.bfloat16), ('row', 'col'), scatter...  32.2 us
    reshape x2, local copies, waits for them, and re-layouts, toeplitz(): skewed = tiled[:, :rows * (width - 1)].reshape(groups, rows, width - 1)  30.6 us
    another operation x4, local copies, waits for them, and re-layouts, toeplitz(): tiled = jnp.tile(seed_row, (1, rows))  29.5 us
    reshape x2, local copies, waits for them, and re-layouts, per_device(): pairs.reshape(ngroups, rows * width)[:, :rows * (width - 1)]  28.4 us
    unnamed x19, local copies, waits for them, and re-layouts  22.2 us
  transfers between devices with their start and end apart: 7, of which 4 were waited for; matrix products, arithmetic and copies ran while one was open for 25% of the time, Pallas kernels for 0%

commit v1 on v0

--- a/solution.py
+++ b/solution.py
@@ -1,7 +1,16 @@
+import functools
 import jax
 import jax.numpy as jnp
 from jax import lax
 from jax.sharding import PartitionSpec as P
+
+
+def arrange_object(raw, chip_axis):
+    parts_out = jnp.concatenate(lax.all_gather(raw, chip_axis), 1)
+    return parts_out
+
+
+serve_the_ways = functools.partial(arrange_object, chip_axis=("row", "col"))
 
 
 def from_behind(block, axis, distance):
@@ -41,7 +50,7 @@
     margin = ntaps - 1
     span = rows + margin
     scale = float(rows * lax.axis_size("dp")) ** (-0.5)
-    whole = lax.all_gather(tokens, ("row", "col"), axis=1, tiled=True)
+    whole = serve_the_ways(tokens)
     full_w = lax.all_gather(in_weight, "dp", axis=0, tiled=True)
     mixed_in = jnp.einsum("sd,dic->sic", whole, full_w, preferred_element_type=jnp.float32).astype(
         jnp.bfloat16

time: 540 us -> 541 us (level)
  transfers between devices with their start and end apart: 7 -> 7, of which waited for: 4 -> 4; matrix products, arithmetic and copies ran while one was open for 25% -> 26% of each run, Pallas kernels for 0% -> 0%
where the time goes in v1:
time: 541 us; the launch traced here: 539 us
  waiting for transfers between devices  196 us (36%)
  local copies, waits for them, and re-layouts  142 us (26%)
  blocking collectives  127 us (23%)
  matrix products  39.5 us (7%)
  between operations  14 us (3%)
  other arithmetic  10.9 us (2%)
  starting transfers between devices  9.64 us (2%)
    psum x1, blocking collectives, per_device(): lax.psum(filter_part.astype(jnp.bfloat16), 'dp').astype(jnp.float32)  127 us
    all_gather x1, waiting for transfers between devices, per_device(): full_w = lax.all_gather(in_weight, 'dp', axis=0, tiled=True)  113 us
    all_gather x1, waiting for transfers between devices, arrange_object(): parts_out = jnp.concatenate(lax.all_gather(raw, chip_axis), 1)  48.7 us
    reduce_scatter x1, waiting for transfers between devices, per_device(): lax.psum_scatter(partial_in.astype(jnp.bfloat16), ('row', 'col'), scatter...  32.1 us
    reshape x2, local copies, waits for them, and re-layouts, toeplitz(): skewed = tiled[:, :rows * (width - 1)].reshape(groups, rows, width - 1)  30.6 us
    another operation x4, local copies, waits for them, and re-layouts, toeplitz(): tiled = jnp.tile(seed_row, (1, rows))  29.5 us
    reshape x2, local copies, waits for them, and re-layouts, per_device(): pairs.reshape(ngroups, rows * width)[:, :rows * (width - 1)]  28.4 us
    unnamed x19, local copies, waits for them, and re-layouts  22.2 us
  transfers between devices with their start and end apart: 7, of which 4 were waited for; matrix products, arithmetic and copies ran while one was open for 26% of the time, Pallas kernels for 0%

profile of v1, /device:TPU:4, one launch (start us, length us, event | category | flops | bytes accessed | tf_op | source)
XLA Modules:
  0.0 539.4 jit_solution(2320550489860452767)
XLA Ops:
  7.2 0.7 all-gather.6.cloned.1.call-update
  7.9 0.7 all-gather.4.cloned.1.call-update
  8.7 48.7 %all-gather.6.cloned.1.call-done = bf16[1536,512]{1,0:T(8,128)(2,1)} async-done(((bf16[192,512]{1,0:T(8,128)(2,1)}), bf16[1536,512]{1,0:T(8,128)(2,1)}) %all-gather.6.cloned.1.call-update) | async-done | bytes 1572880 | tf_op jit(solution)/shard_map/all_gather | solution.py:9
  57.4 2.3 copy.40
  59.7 2.1 reshape.66
  61.8 112.8 %all-gather.4.cloned.1.call-done = bf16[4096,3,512]{2,0,1:T(8,128)(2,1)} async-done(((bf16[128,3,512]{2,0,1:T(8,128)(2,1)}), bf16[4096,3,512]{2,0,1:T(8,128)(2,1)}) %all-gather.4.cloned.1.call-update) | async-done | bytes 12582928 | tf_op jit(solution)/shard_map/all_gather | solution.py:54
  174.6 7.7 %convolution_convert_fusion = bf16[192,3,512]{2,0,1:T(8,128)(2,1)S(1)} fusion(bf16[192,4096,1]{1,0,2:T(8,128)(2,1)} %reshape.66, bf16[4096,3,512]{2,0,1:T(8,128)(2,1)} %all-gather.4.cloned.1.call-done), kind=kOutput, calls=%fused_computation.14 | convolution fusion | flops 2416214016 | bytes 14745600 | tf_op jit(solution)/shard_map/sd,dic->sic/dot_general | solution.py:55
  182.4 2.2 collective-permute-start
  184.7 3.1 tile.8
  187.8 11.6 %tile.9 = bf16[32,98112]{1,0:T(8,128)(2,1)} reshape(bf16[32,192,511]{2,1,0:T(8,128)(2,1)} %tile.8) | data formatting | bytes 12558336 | tf_op jit(solution)/shard_map/tile | solution.py:28
  199.4 5.8 %slice.119 = bf16[32,97920]{1,0:T(8,128)(2,1)} slice(bf16[32,98112]{1,0:T(8,128)(2,1)} %tile.9), slice={[0:32], [0:97920]} | slice | bytes 12533760 | tf_op jit(solution)/shard_map/slice | solution.py:29
  205.2 15.3 %reshape.57 = bf16[32,192,510]{2,1,0:T(8,128)(2,1)} reshape(bf16[32,97920]{1,0:T(8,128)(2,1)} %slice.119) | data formatting | bytes 12533760 | tf_op jit(solution)/shard_map/reshape | solution.py:29
  220.6 0.3 maximum_convert_fusion
  220.9 0.6 fusion.5
  221.5 1.3 copy-done
  223.1 4.1 fusion.3
  227.2 0.9 copy.28
  228.1 1.9 fusion.17
  230.0 5.1 collective-permute-start.1
  235.2 3.2 tile.20
  238.3 11.6 %tile.21 = bf16[32,98112]{1,0:T(8,128)(2,1)} reshape(bf16[32,192,511]{2,1,0:T(8,128)(2,1)} %tile.20) | data formatting | bytes 12558336 | tf_op jit(solution)/shard_map/tile | solution.py:28
  249.9 5.8 %slice.122 = bf16[32,97920]{1,0:T(8,128)(2,1)} slice(bf16[32,98112]{1,0:T(8,128)(2,1)} %tile.21), slice={[0:32], [0:97920]} | slice | bytes 12533760 | tf_op jit(solution)/shard_map/slice | solution.py:29
  255.8 15.3 %reshape.60 = bf16[32,192,510]{2,1,0:T(8,128)(2,1)} reshape(bf16[32,97920]{1,0:T(8,128)(2,1)} %slice.122) | data formatting | bytes 12533760 | tf_op jit(solution)/shard_map/reshape | solution.py:29
  271.1 0.9 copy.30
  272.0 4.2 fusion.1
  276.2 0.9 copy.31
  277.2 1.4 slice_multiply_fusion.10
  278.7 2.0 collective-permute-start.2
  280.7 1.4 collective-permute-done.2
  282.2 0.8 fusion.9
  283.0 0.6 copy-done.1
  283.6 6.6 %multiply_convert_fusion = bf16[3,512,4096]{2,1,0:T(8,128)(2,1)} fusion(bf16[192,3,512]{2,0,1:T(8,128)(2,1)S(1)} %get-tuple-element.29, bf16[192,4096,1]{1,0,2:T(8,128)(2,1)S(1)} %copy-done.1), kind=kOutput, calls=%fused_computation | convolution fusion | flops 2428502016 | bytes 14745600 | tf_op jit(solution)/shard_map/sd,sic->dic/dot_general | solution.py:128
  290.2 16.6 %copy.37 = bf16[4096,1536]{1,0:T(8,128)(2,1)} copy(bf16[4096,1536]{0,1:T(8,128)(2,1)} %bitcast.61) | data formatting | bytes 25165824
  306.9 0.3 reduce-scatter.5.cloned.1.call-start
  307.1 0.8 copy-done.3
  307.9 10.0 %fusion = bf16[192,4096]{1,0:T(8,128)(2,1)} fusion(bf16[192,3,512]{2,0,1:T(8,128)(2,1)S(1)} %copy-done.3, bf16[4096,3,512]{2,0,1:T(8,128)(2,1)} %all-gather.4.cloned.1.call-done), kind=kOutput, calls=%fused_computation.2 | convolution fusion | flops 2416705536 | bytes 14745600 | tf_op jit(solution)/shard_map/sic,dic->sd/dot_general | solution.py:123
  318.1 0.5 reverse
  318.8 6.9 %fusion.14 = f32[32,192,511]{2,1,0:T(8,128)} fusion(bf16[32,16,192]{2,1,0:T(8,128)(2,1)S(1)} %bitcast.70, bf16[32,16,319]{2,1,0:T(8,128)(2,1)S(1)} %slice.183), kind=kOutput, calls=%fused_computation.31 | convolution fusion | flops 100466688 | bytes 13081600 | tf_op jit(solution)/shard_map/gcs,gcu->gsu/dot_general | solution.py:92
  325.7 13.2 %reshape.63 = f32[32,98112]{1,0:T(8,128)} reshape(f32[32,192,511]{2,1,0:T(8,128)} %fusion.14) | data formatting | bytes 25116672 | tf_op jit(solution)/shard_map/reshape | solution.py:98
  338.8 11.4 %slice.129 = f32[32,97920]{1,0:T(8,128)} slice(f32[32,98112]{1,0:T(8,128)} %reshape.63), slice={[0:32], [0:97920]} | slice | bytes 25067520 | tf_op jit(solution)/shard_map/slice | solution.py:98
  350.3 15.2 %reshape.64 = f32[32,192,510]{2,1,0:T(8,128)} reshape(f32[32,97920]{1,0:T(8,128)} %slice.129) | data formatting | bytes 25067520 | tf_op jit(solution)/shard_map/reshape | solution.py:98
  365.5 4.4 slice_reduce_fusion
  369.9 127.3 %all-reduce.3 = (bf16[32,128]{1,0:T(8,128)(2,1)S(1)}, bf16[3,3,512]{2,1,0:T(4,128)(2,1)S(1)}) all-reduce(bf16[32,128]{1,0:T(8,128)(2,1)S(1)} %slice_reduce_fusion, bf16[3,3,512]{2,1,0:T(4,128)(2,1)S(1)} %pad_maximum_fusion.3), channel_id=1, replica_groups=mesh['dp'=32,'row'=4,'col'=2] {'dp'}, use_global_device_ids=true, to_apply=%region_3.0 | all-reduce | flops 8704 | bytes 34816 | tf_op jit(solution)/shard_map/psum | solution.py:118
  497.3 0.6 convert_multiply_fusion.3
  497.9 0.6 convert_multiply_fusion.2
  498.5 1.2 copy.38
  499.7 1.1 copy.34
  500.8 32.1 %reduce-scatter.5.cloned.1.call-done = bf16[192,512]{1,0:T(8,128)(2,1)} async-done(((bf16[192,4096]{1,0:T(8,128)(2,1)}), bf16[192,512]{1,0:T(8,128)(2,1)}) %reduce-scatter.5.cloned.1.call-update) | async-done | bytes 196624 | tf_op jit(solution)/shard_map/reduce_scatter | solution.py:124
  (34 shorter events, 1.3 us)
Async XLA Ops:
  7.2 50.3 %all-gather.6.cloned.1.call-start = ((), (), s32[]{:S(2)}) async-start(), calls=%async_computation.4 | async-start | bytes 1769472 | tf_op jit(solution)/shard_map/all_gather | solution.py:9
  7.9 166.7 %all-gather.4.cloned.1.call-start = ((), (), s32[]{:S(2)}) async-start(), calls=%async_computation.2 | async-start | bytes 12976128 | tf_op jit(solution)/shard_map/all_gather | solution.py:54
  8.6 489.8 %reduce-scatter.7.cloned.1.call-start = ((), (), s32[]{:S(2)}) async-start(), calls=%async_computation.5 | async-start | bytes 12976128
  61.8 122.7 %copy-start.5 = (bf16[32,128]{1,0:T(8,128)(2,1)S(1)}, bf16[32,128]{1,0:T(8,128)(2,1)}, u32[]{:S(2)}) copy-start(bf16[32,128]{1,0:T(8,128)(2,1)} %param.8) | copy-start | bytes 24580
  182.4 38.2 %collective-permute-start = (bf16[129,3,512]{2,0,1:T(8,128)(2,1)S(1)}, bf16[129,3,512]{2,0,1:T(8,128)(2,1)S(1)}, u32[]{:S(2)}, u32[]{:S(2)}) collective-permute-start(bf16[129,3,512]{2,0,1:T(8,128)(2,1)S(1)} %slice.112), channel_id=1, source_target_pairs={{0,8},{8,16},{16,24},{24,32},{32,40},{40,48},{48,56},{56,64},{64,7... | collective-permute-start | bytes 1188872 | tf_op jit(solution)/shard_map/ppermute | solution.py:19
  205.2 15.3 %copy-start.6 = (f32[3,3,512]{2,1,0:T(4,128)S(1)}, f32[3,3,512]{2,1,0:T(4,128)}, u32[]{:S(2)}) copy-start(f32[3,3,512]{2,1,0:T(4,128)} %param.7) | copy-start | bytes 55300
  221.4 1.3 copy-start
  223.1 5.1 copy-start.4
  230.0 41.0 %collective-permute-start.1 = (bf16[127,512]{1,0:T(8,128)(2,1)S(1)}, bf16[127,512]{1,0:T(8,128)(2,1)S(1)}, u32[]{:S(2)}, u32[]{:S(2)}) collective-permute-start(bf16[127,512]{1,0:T(8,128)(2,1)S(1)} %slice.121), channel_id=1, source_target_pairs={{8,0},{16,8},{24,16},{32,24},{40,32},{48,40},{56,48},{64,56},{72,6... | collective-permute-start | bytes 390152 | tf_op jit(solution)/shard_map/ppermute | solution.py:19
  278.7 3.4 collective-permute-start.2
  282.2 1.4 copy-start.1
  283.0 7.2 %copy-start.2 = (bf16[192,3,512]{2,0,1:T(8,128)(2,1)}, bf16[192,3,512]{2,0,1:T(8,128)(2,1)S(1)}, u32[]{:S(2)}) copy-start(bf16[192,3,512]{2,0,1:T(8,128)(2,1)S(1)} %get-tuple-element.29) | copy-start | bytes 1769476
  306.9 1.1 copy-start.3
  306.9 226.0 %reduce-scatter.5.cloned.1.call-start = ((), (), s32[]{:S(2)}) async-start(), calls=%async_computation.3 | async-start | bytes 1769472 | tf_op jit(solution)/shard_map/reduce_scatter | solution.py:124
Sparse Core Ops, SparseCore 0:
  9.8 47.6 all-gather.5
  60.2 114.3 all-gather.3
  307.0 175.6 reduce-scatter.6
  485.7 47.1 reduce-scatter.4
